TPU v7x, 32 devices: a whole 2x2x4 slice. The times are simulated.
32 devices in a mesh: ctx: 8 (over y, x, core), head: 4 (over z).
Axes of the slice: x: 2, y: 2, z: 4, core: 2. Of those that a mesh axis runs over, the one named last changes fastest.
Arguments:
- queries: bfloat16 [2048, 4096], P('ctx', 'head'), may hold values from -6 to 6
- key_rows: bfloat16 [2048, 4096], P('ctx', 'head'), may hold values from -6 to 6
- value_rows: bfloat16 [2048, 4096], P('ctx', 'head'), may hold values from -6 to 6
- out_weight: bfloat16 [4096, 4096], P('head'), may hold values from -0.125 to 0.125
- cotangent: bfloat16 [2048, 4096], P('ctx', 'head'), may hold values from -6 to 6
Outputs:
- mixed: bfloat16 [2048, 4096], P('ctx', 'head')
- grad_queries: bfloat16 [2048, 4096], P('ctx', 'head')
- grad_keys: bfloat16 [2048, 4096], P('ctx', 'head')
- grad_values: bfloat16 [2048, 4096], P('ctx', 'head')
- grad_out_weight: float32 [4096, 4096], P('head', 'ctx')
All inputs are finite; a program needn't handle non-finite values.
Results may differ from a plain program's by a relative error of at most 0.0052.
Values may be sent and summed in bfloat16 or wider, within the bound.
No kernel may reach another device: no remote copies, remote signals or barrier semaphores. Data moves between devices by JAX's collectives and lax.ppermute only.
A program may use at most 64 MiB of HBM per device.

v0:
```python
import jax
import jax.numpy as jnp
from jax import lax
from jax.sharding import PartitionSpec as P

HEAD_DIM = 128
epsilon = 1e-06


def compensated(earlier, later):
    first_sum, first_comp = earlier
    second_sum, second_comp = later
    error_term = first_sum - (second_sum - second_sum) + (second_sum - second_sum)
    return (second_sum, error_term)


def fold_masked(heads_here, position, lower, running, portion):
    count = portion.shape[0] // heads_here
    owners = jnp.arange(count, dtype=jnp.int32)
    keep_mask = owners < position if lower else owners > position
    weights = keep_mask.astype(jnp.float32)
    blocks = portion.reshape((count, heads_here) + portion.shape[1:])
    added_part = jnp.sum(blocks * weights[:, None, None, None], axis=0)
    return compensated(running, (added_part, jnp.zeros_like(added_part)))


def body(queries, key_rows, value_rows, out_weight, cotangent):
    length = queries.shape[0]
    heads_here = queries.shape[1] // HEAD_DIM
    width_here = heads_here * HEAD_DIM
    highest = lax.Precision.HIGHEST
    query_three = queries.reshape(length, heads_here, HEAD_DIM)
    key_three = key_rows.reshape(length, heads_here, HEAD_DIM)
    value_three = value_rows.reshape(length, heads_here, HEAD_DIM)
    causal = lax.broadcasted_iota(jnp.int32, (length, length), 0) >= lax.broadcasted_iota(
        jnp.int32, (length, length), 1
    )
    position = lax.axis_index("ctx")
    scores = jnp.einsum("thd,shd->hts", query_three, key_three, preferred_element_type=jnp.float32)
    scores = jnp.where(causal[None], scores, 0.0).astype(jnp.bfloat16)
    block_state = jnp.einsum(
        "thd,the->hde", key_three, value_three, preferred_element_type=jnp.float32
    )
    zero_state = jnp.zeros_like(block_state)
    prefix_sums, prefix_comps = fold_masked(
        heads_here,
        position,
        True,
        (zero_state, zero_state),
        lax.all_gather(block_state, "ctx", axis=0, tiled=True),
    )
    prefix_state = prefix_sums + prefix_comps
    query_wide = query_three.astype(jnp.float32)
    attended = jnp.einsum("hts,she->the", scores, value_three, preferred_element_type=jnp.float32)
    attended = attended + jnp.einsum("thd,hde->the", query_wide, prefix_state, precision=highest)
    row_scale = lax.rsqrt(jnp.mean(attended * attended, axis=-1, keepdims=True) + epsilon)
    unit_rows = attended * row_scale
    normed = unit_rows.astype(jnp.bfloat16).reshape(length, width_here)
    partial_terms = jnp.dot(normed, out_weight, preferred_element_type=jnp.float32)
    mixed = lax.psum_scatter(partial_terms, "head", scatter_dimension=1, tiled=True).astype(
        jnp.bfloat16
    )
    full_grad = lax.all_gather(cotangent, "head", axis=1, tiled=True)
    upstream = lax.dot_general(
        full_grad, out_weight, (((1,), (1,)), ((), ())), preferred_element_type=jnp.float32
    )
    upstream = upstream.reshape(length, heads_here, HEAD_DIM)
    d_attended = row_scale * (
        upstream - unit_rows * jnp.mean(upstream * unit_rows, axis=-1, keepdims=True)
    )
    d_attended = d_attended.astype(jnp.bfloat16)
    grad_block = jnp.einsum(
        "thd,the->hde", query_three, d_attended, preferred_element_type=jnp.float32
    )
    suffix_sums, suffix_comps = fold_masked(
        heads_here,
        position,
        False,
        (zero_state, zero_state),
        lax.all_gather(grad_block, "ctx", axis=0, tiled=True),
    )
    suffix_state = suffix_sums + suffix_comps
    back_scores = jnp.einsum(
        "the,she->hts", d_attended, value_three, preferred_element_type=jnp.float32
    )
    back_scores = jnp.where(causal[None], back_scores, 0.0).astype(jnp.bfloat16)
    grad_wide = d_attended.astype(jnp.float32)
    grad_q = jnp.einsum("hts,shd->thd", back_scores, key_three, preferred_element_type=jnp.float32)
    grad_q = grad_q + jnp.einsum("the,hde->thd", grad_wide, prefix_state, precision=highest)
    grad_k = jnp.einsum(
        "hts,thd->shd", back_scores, query_three, preferred_element_type=jnp.float32
    )
    grad_k = grad_k + jnp.einsum(
        "she,hde->shd", value_three.astype(jnp.float32), suffix_state, precision=highest
    )
    grad_v = jnp.einsum("hts,the->she", scores, d_attended, preferred_element_type=jnp.float32)
    grad_v = grad_v + jnp.einsum(
        "shd,hde->she", key_three.astype(jnp.float32), suffix_state, precision=highest
    )
    grad_cols = lax.all_to_all(full_grad, "ctx", split_axis=1, concat_axis=0, tiled=True)
    grad_out_weight = lax.dot_general(
        lax.all_gather(normed, "ctx", axis=0, tiled=True),
        grad_cols,
        (((0,), (0,)), ((), ())),
        preferred_element_type=jnp.float32,
    )
    return (
        mixed,
        grad_q.astype(jnp.bfloat16).reshape(length, width_here),
        grad_k.astype(jnp.bfloat16).reshape(length, width_here),
        grad_v.astype(jnp.bfloat16).reshape(length, width_here),
        grad_out_weight,
    )


def solution(mesh):
    return jax.shard_map(
        body,
        mesh=mesh,
        in_specs=(
            P("ctx", "head"),
            P("ctx", "head"),
            P("ctx", "head"),
            P("head", None),
            P("ctx", "head"),
        ),
        out_specs=(
            P("ctx", "head"),
            P("ctx", "head"),
            P("ctx", "head"),
            P("ctx", "head"),
            P("head", "ctx"),
        ),
        check_vma=False,
    )
```

profile of v0, /device:TPU:0, one launch (start us, length us, event | category | flops | bytes accessed | tf_op | source)
XLA Modules:
  0.0 284.7 jit_solution(707623122106704745)
XLA Ops:
  7.3 1.3 copy.103
  8.9 2.1 fusion.11
  11.1 1.0 copy.79
  12.7 1.0 copy-done.5
  13.7 1.5 convolution_bitcast_fusion.5
  15.1 35.4 %all-gather.5.cloned.1.call-done = f32[64,128,128]{2,1,0:T(8,128)} async-done(((f32[8,128,128]{2,1,0:T(8,128)}), f32[64,128,128]{2,1,0:T(8,128)}) %all-gather.5.cloned.1.call-update) | async-done | bytes 4194320 | tf_op jit(solution)/shard_map/all_gather | solution.py:50
  50.5 2.8 multiply_reduce_fusion.1
  53.3 0.8 copy-done.2
  54.1 0.7 multiply_reduce_fusion.3
  54.9 43.5 %all-gather.7.cloned.1.call-done = bf16[256,4096]{0,1:T(8,128)(2,1)} async-done(((bf16[256,1024]{0,1:T(8,128)(2,1)}), bf16[256,4096]{0,1:T(8,128)(2,1)}) %all-gather.7.cloned.1.call-update) | async-done | bytes 2097168 | tf_op jit(solution)/shard_map/all_gather | solution.py:63
  98.3 6.3 %multiply_reduce_fusion.2 = (f32[256,8]{0,1:T(8,128)S(1)}, f32[256,1024]{0,1:T(8,128)S(1)}) fusion(f32[256,8,128]{0,2,1:T(8,128)S(1)} %get-tuple-element.28, f32[256,8]{0,1:T(8,128)S(1)} %add_rsqrt_fusion, bf16[1024,4096]{1,0:T(8,128)(2,1)} %param.8, bf16[256,4096]{0,1:T(8,128)(2,1)} %all-gather.7.cloned.1.call-done), kind=kOutput, calls=%fused_computation.19 | convolution fusion | flops 2148268032 | bytes 12599296 | tf_op jit(solution)/shard_map/dot_general | solution.py:64
  104.6 1.0 multiply_convert_fusion
  106.0 1.0 copy.87
  107.0 0.5 all-gather.11.cloned.1.call-update
  107.6 7.9 %fusion.41 = f32[256,4096]{1,0:T(8,128)} fusion(bf16[256,1024]{0,1:T(8,128)(2,1)} %bitcast.115, bf16[1024,4096]{1,0:T(8,128)(2,1)} %param.8), kind=kOutput, calls=%fused_computation.60 | convolution fusion | flops 2147483648 | bytes 13107200 | tf_op jit(solution)/shard_map/dot_general | solution.py:59
  115.6 4.6 %all-to-all-start = ((bf16[256,8,512]{0,2,1:T(8,128)(2,1)}), bf16[256,8,512]{0,2,1:T(8,128)(2,1)}, u32[]{:S(2)}, u32[]{:S(2)}) async-start(bf16[256,8,512]{0,2,1:T(8,128)(2,1)} %bitcast.15), calls=%async_computation.1 | async-start | bytes 4194304 | tf_op jit(solution)/shard_map/all_to_all | solution.py:100
  120.1 36.2 %all-to-all-done = bf16[256,8,512]{0,2,1:T(8,128)(2,1)} async-done(((bf16[256,8,512]{0,2,1:T(8,128)(2,1)}), bf16[256,8,512]{0,2,1:T(8,128)(2,1)}, u32[]{:S(2)}, u32[]{:S(2)}) %all-to-all-start) | async-done | bytes 2097184 | tf_op jit(solution)/shard_map/all_to_all | solution.py:100
  156.4 4.0 %copy.91 = bf16[8,256,512]{2,1,0:T(8,128)(2,1)} copy(bf16[8,256,512]{1,2,0:T(8,128)(2,1)} %bitcast.16) | data formatting | bytes 4194304 | tf_op jit(solution)/shard_map/all_to_all | solution.py:100
  160.3 0.5 select_convert_fusion
  161.3 0.6 fusion.3
  161.9 1.0 copy.92
  162.9 2.5 fusion.42
  165.4 1.7 convolution_bitcast_fusion.3
  167.2 3.0 %multiply_reduce_fusion = f32[8,128,128]{2,1,0:T(8,128)S(1)} fusion(f32[8,8,128,128]{3,2,1,0:T(8,128)} %bitcast.116, f32[8]{0:T(128)S(1)} %compare_convert_fusion), kind=kLoop, calls=%fused_computation | loop fusion | flops 1966080 | bytes 4718624 | tf_op jit(solution)/shard_map/reduce_sum | solution.py:23
  170.2 1.4 fusion.5
  171.6 2.0 copy.94
  173.7 0.6 fusion.4
  174.3 1.0 copy.93
  175.3 21.8 %all-gather.11.cloned.1.call-done = bf16[2048,1024]{0,1:T(8,128)(2,1)} async-done(((bf16[256,1024]{0,1:T(8,128)(2,1)}), bf16[2048,1024]{0,1:T(8,128)(2,1)}) %all-gather.11.cloned.1.call-update) | async-done | bytes 4194320 | tf_op jit(solution)/shard_map/all_gather | solution.py:102
  197.1 6.5 %fusion.43 = f32[1024,512]{1,0:T(8,128)} fusion(bf16[2048,1024]{0,1:T(8,128)(2,1)} %all-gather.11.cloned.1.call-done, bf16[2048,512]{1,0:T(8,128)(2,1)} %bitcast.122), kind=kOutput, calls=%fused_computation.62 | convolution fusion | flops 2147483648 | bytes 8388608 | tf_op jit(solution)/shard_map/dot_general | solution.py:101
  203.6 72.5 %reduce-scatter.2.cloned.1.call-done = f32[256,1024]{1,0:T(8,128)} async-done(((f32[256,4096]{1,0:T(8,128)}), f32[256,1024]{1,0:T(8,128)}) %reduce-scatter.2.cloned.1.call-update) | async-done | bytes 1048592 | tf_op jit(solution)/shard_map/reduce_scatter | solution.py:60
  276.1 2.1 convert_element_type.48
  (39 shorter events, 1.9 us)
Async XLA Ops:
  7.2 5.0 %copy-start = (bf16[256,1024]{1,0:T(8,128)(2,1)S(1)}, bf16[256,1024]{1,0:T(8,128)(2,1)}, u32[]{:S(2)}) copy-start(bf16[256,1024]{1,0:T(8,128)(2,1)} %param.5) | copy-start | bytes 1572868
  7.2 5.0 %copy-start.8 = (bf16[256,1024]{1,0:T(8,128)(2,1)S(1)}, bf16[256,1024]{1,0:T(8,128)(2,1)}, u32[]{:S(2)}) copy-start(bf16[256,1024]{1,0:T(8,128)(2,1)} %param.6) | copy-start | bytes 1572868
  7.2 3.9 %copy-start.10 = (bf16[256,1024]{1,0:T(8,128)(2,1)S(1)}, bf16[256,1024]{1,0:T(8,128)(2,1)}, u32[]{:S(2)}) copy-start(bf16[256,1024]{1,0:T(8,128)(2,1)} %param.9) | copy-start | bytes 1572868
  7.2 43.3 %all-gather.5.cloned.1.call-start = ((), (), s32[]{:S(2)}) async-start(), calls=%async_computation.2 | async-start | bytes 4718592 | tf_op jit(solution)/shard_map/all_gather | solution.py:50
  7.2 6.4 %copy-start.1 = (bf16[256,1024]{1,0:T(8,128)(2,1)S(1)}, bf16[256,1024]{1,0:T(8,128)(2,1)}, u32[]{:S(2)}) copy-start(bf16[256,1024]{1,0:T(8,128)(2,1)} %param.7) | copy-start | bytes 1572868
  11.0 87.3 %all-gather.7.cloned.1.call-start = ((), (), s32[]{:S(2)}) async-start(), calls=%async_computation.4 | async-start | bytes 2621440 | tf_op jit(solution)/shard_map/all_gather | solution.py:63
  12.1 155.0 %all-gather.9.cloned.1.call-start = ((), (), s32[]{:S(2)}) async-start(), calls=%async_computation.5 | async-start | bytes 4718592 | tf_op jit(solution)/shard_map/all_gather | solution.py:80
  12.7 1.0 copy-start.5
  50.5 3.6 %copy-start.4 = (f32[256,8,128]{0,2,1:T(8,128)S(1)}, f32[256,8,128]{0,2,1:T(8,128)}, u32[]{:S(2)}) copy-start(f32[256,8,128]{0,2,1:T(8,128)} %convolution_bitcast_fusion.5) | copy-start | bytes 3145732
  53.3 0.8 copy-start.2
  107.0 90.1 %all-gather.11.cloned.1.call-start = ((), (), s32[]{:S(2)}) async-start(), calls=%async_computation.6 | async-start | bytes 4718592 | tf_op jit(solution)/shard_map/all_gather | solution.py:102
  107.6 168.5 %reduce-scatter.2.cloned.1.call-start = ((), (), s32[]{:S(2)}) async-start(), calls=%async_computation.3 | async-start | bytes 5242880 | tf_op jit(solution)/shard_map/reduce_scatter | solution.py:60
  115.6 40.8 %all-to-all-start = ((bf16[256,8,512]{0,2,1:T(8,128)(2,1)}), bf16[256,8,512]{0,2,1:T(8,128)(2,1)}, u32[]{:S(2)}, u32[]{:S(2)}) async-start(bf16[256,8,512]{0,2,1:T(8,128)(2,1)} %bitcast.15), calls=%async_computation.1 | async-start | bytes 4194304 | tf_op jit(solution)/shard_map/all_to_all | solution.py:100
  156.4 4.9 %copy-start.3 = (f32[8,128,128]{2,1,0:T(8,128)S(1)}, f32[8,128,128]{2,1,0:T(8,128)}, u32[]{:S(2)}) copy-start(f32[8,128,128]{2,1,0:T(8,128)} %copy-done.2) | copy-start | bytes 1572868
  160.8 1.1 copy-start.6
  165.4 4.7 %copy-start.9 = (bf16[256,1024]{1,0:T(8,128)(2,1)S(1)}, bf16[256,1024]{1,0:T(8,128)(2,1)}, u32[]{:S(2)}) copy-start(bf16[256,1024]{1,0:T(8,128)(2,1)} %param.6) | copy-start | bytes 1572868
  167.2 3.0 %copy-start.7 = (f32[8,128,256]{2,1,0:T(8,128)S(1)}, f32[8,128,256]{2,1,0:T(8,128)}, u32[]{:S(2)}) copy-start(f32[8,128,256]{2,1,0:T(8,128)} %fusion.42) | copy-start | bytes 3145732
Sparse Core Ops, SparseCore 0:
  11.1 39.2 all-gather.4
  52.6 45.6 all-gather.6
  107.1 51.2 all-gather.8
  160.8 36.3 all-gather.10
  199.2 76.7 reduce-scatter.1
where the time goes:
time: 285 us
  waiting for transfers between devices  210 us (74%)
  matrix products  33.5 us (12%)
  between operations  14 us (5%)
  local copies, waits for them, and re-layouts  13.4 us (5%)
  other arithmetic  9 us (3%)
  starting transfers between devices  4.77 us (2%)
    reduce_scatter x1, waiting for transfers between devices, body(): lax.psum_scatter(partial_terms, 'head', scatter_dimension=1, tiled=True)  72.5 us
    all_gather x1, waiting for transfers between devices, body(): full_grad = lax.all_gather(cotangent, 'head', axis=1, tiled=True)  43.5 us
    all_to_all x1, waiting for transfers between devices, body(): lax.all_to_all(full_grad, 'ctx', split_axis=1, concat_axis=0, tiled=True)  36.2 us
    all_gather x1, waiting for transfers between devices, body(): lax.all_gather(block_state, 'ctx', axis=0, tiled=True)  35.4 us
    all_gather x1, waiting for transfers between devices, body(): lax.all_gather(normed, 'ctx', axis=0, tiled=True)  21.8 us
    unnamed x27, local copies, waits for them, and re-layouts  8.13 us
    dot_general x1, matrix products, body(): jnp.dot(normed, out_weight, preferred_element_type=jnp.float32)  7.92 us
    dot_general x1, matrix products, body(): lax.dot_general(lax.all_gather(normed, 'ctx', axis=0, tiled=True), grad_c...  6.51 us
  transfers between devices with their start and end apart: 6, of which 5 were waited for; matrix products, arithmetic and copies ran while one was open for 14% of the time, Pallas kernels for 0%

commit v1 on v0

--- a/solution.py
+++ b/solution.py
@@ -60,7 +60,12 @@
     mixed = lax.psum_scatter(partial_terms, "head", scatter_dimension=1, tiled=True).astype(
         jnp.bfloat16
     )
-    full_grad = lax.all_gather(cotangent, "head", axis=1, tiled=True)
+    ring = [cotangent]
+    for hop in range(3):
+        ring.append(lax.ppermute(ring[-1], "head", [(dev, (dev + 1) % 4) for dev in range(4)]))
+    full_grad = jnp.roll(
+        jnp.concatenate(ring[::-1], axis=1), (lax.axis_index("head") + 1) * ring[0].shape[1], axis=1
+    )
     upstream = lax.dot_general(
         full_grad, out_weight, (((1,), (1,)), ((), ())), preferred_element_type=jnp.float32
     )

time: 285 us -> 252 us (0.88)
  waiting for transfers between devices: 210 us -> 173 us
    all_gather x1 -> x0, waiting for transfers between devices: 43.5 us -> none  [body(): full_grad = lax.all_gather(cotangent, 'head', axis=1, tiled=True)]
    ppermute x0 -> x3, waiting for transfers between devices: none -> 42.1 us  [body(): lax.ppermute(ring[-1], 'head', [(dev, (dev + 1) % 4) for dev in range(4)])]
    all_gather x1, waiting for transfers between devices: 35.4 us -> 0.01 us  [body(): lax.all_gather(block_state, 'ctx', axis=0, tiled=True)]
    ppermute x0 -> x3, starting transfers between devices: none -> 3.11 us  [body(): lax.ppermute(ring[-1], 'head', [(dev, (dev + 1) % 4) for dev in range(4)])]
    unnamed x27 -> x42, local copies, waits for them, and re-layouts: 8.13 us -> 8.73 us
  transfers between devices with their start and end apart: 6 -> 8, of which waited for: 5 -> 6; matrix products, arithmetic and copies ran while one was open for 14% -> 15% of each run, Pallas kernels for 0% -> 0%
where the time goes in v1:
time: 252 us; the launch traced here: 251 us
  waiting for transfers between devices  173 us (69%)
  matrix products  34.1 us (14%)
  between operations  14.1 us (6%)
  local copies, waits for them, and re-layouts  14 us (6%)
  other arithmetic  9.07 us (4%)
  starting transfers between devices  7.07 us (3%)
    reduce_scatter x1, waiting for transfers between devices, body(): lax.psum_scatter(partial_terms, 'head', scatter_dimension=1, tiled=True)  72.5 us
    ppermute x3, waiting for transfers between devices, body(): lax.ppermute(ring[-1], 'head', [(dev, (dev + 1) % 4) for dev in range(4)])  42.1 us
    all_to_all x1, waiting for transfers between devices, body(): lax.all_to_all(full_grad, 'ctx', split_axis=1, concat_axis=0, tiled=True)  34.3 us
    all_gather x1, waiting for transfers between devices, body(): lax.all_gather(normed, 'ctx', axis=0, tiled=True)  23.4 us
    unnamed x42, local copies, waits for them, and re-layouts  8.73 us
    dot_general x1, matrix products, body(): jnp.dot(normed, out_weight, preferred_element_type=jnp.float32)  7.9 us
    dot_general x1, matrix products, body(): lax.dot_general(lax.all_gather(normed, 'ctx', axis=0, tiled=True), grad_c...  6.51 us
    dot_general x1, matrix products, body(): lax.dot_general(full_grad, out_weight, (((1,), (1,)), ((), ())), preferre...  6.32 us
  transfers between devices with their start and end apart: 8, of which 6 were waited for; matrix products, arithmetic and copies ran while one was open for 15% of the time, Pallas kernels for 0%

profile of v1, /device:TPU:0, one launch (start us, length us, event | category | flops | bytes accessed | tf_op | source)
XLA Modules:
  0.0 251.5 jit_solution(582030419039595638)
XLA Ops:
  7.3 1.3 copy.107
  8.9 2.3 fusion.11
  11.5 3.1 %collective-permute-start = (bf16[256,1024]{0,1:T(8,128)(2,1)S(1)}, bf16[256,1024]{0,1:T(8,128)(2,1)S(1)}, u32[]{:S(2)}, u32[]{:S(2)}) collective-permute-start(bf16[256,1024]{0,1:T(8,128)(2,1)S(1)} %copy.81), channel_id=1, source_target_pairs={{0,1},{1,2},{2,3},{3,0},{4,5},{5,6},{6,7},{7,4},{8,9},{9,10},{10,1... | collective-permute-start | bytes 1572872 | tf_op jit(solution)/shard_map/ppermute | solution.py:65
  14.6 13.9 %collective-permute-done = bf16[256,1024]{0,1:T(8,128)(2,1)S(1)} collective-permute-done((bf16[256,1024]{0,1:T(8,128)(2,1)S(1)}, bf16[256,1024]{0,1:T(8,128)(2,1)S(1)}, u32[]{:S(2)}, u32[]{:S(2)}) %collective-permute-start) | collective-permute-done | bytes 524320 | tf_op jit(solution)/shard_map/ppermute | solution.py:65
  28.6 14.9 %collective-permute-done.1 = bf16[256,1024]{0,1:T(8,128)(2,1)} collective-permute-done((bf16[256,1024]{0,1:T(8,128)(2,1)S(1)}, bf16[256,1024]{0,1:T(8,128)(2,1)}, u32[]{:S(2)}, u32[]{:S(2)}) %collective-permute-start.1) | collective-permute-done | bytes 524320 | tf_op jit(solution)/shard_map/ppermute | solution.py:65
  44.6 13.2 %collective-permute-done.2 = bf16[256,1024]{0,1:T(8,128)(2,1)S(1)} collective-permute-done((bf16[256,1024]{0,1:T(8,128)(2,1)}, bf16[256,1024]{0,1:T(8,128)(2,1)S(1)}, u32[]{:S(2)}, u32[]{:S(2)}) %collective-permute-start.2) | collective-permute-done | bytes 524320 | tf_op jit(solution)/shard_map/ppermute | solution.py:65
  57.8 1.1 constant_dynamic-update-slice_fusion.6
  59.0 1.1 constant_dynamic-update-slice_fusion.2
  60.2 1.5 constant_dynamic-slice_fusion
  61.7 2.8 %multiply_reduce_fusion.1 = f32[8,128,128]{2,1,0:T(8,128)S(1)} fusion(f32[8,8,128,128]{3,2,1,0:T(8,128)} %bitcast.117, f32[8]{0:T(128)S(1)} %compare_convert_fusion.1), kind=kLoop, calls=%fused_computation.1 | loop fusion | flops 1966080 | bytes 4718624 | tf_op jit(solution)/shard_map/reduce_sum | solution.py:23
  64.5 0.8 copy-done.4
  65.3 0.7 multiply_reduce_fusion.3
  66.0 6.3 %multiply_reduce_fusion.2 = (f32[256,8]{0,1:T(8,128)S(1)}, f32[256,1024]{0,1:T(8,128)S(1)}) fusion(f32[256,8,128]{0,2,1:T(8,128)S(1)} %get-tuple-element.28, f32[256,8]{0,1:T(8,128)S(1)} %add_rsqrt_fusion, bf16[1024,4096]{1,0:T(8,128)(2,1)} %param.8, bf16[256,4096]{0,1:T(8,128)(2,1)} %constant_dynamic-slice_fusion), kind=kOutput, calls=%fused_computation.19 | convolution fusion | flops 2148268032 | bytes 12599296 | tf_op jit(solution)/shard_map/dot_general | solution.py:69
  72.3 1.0 multiply_convert_fusion
  73.6 1.0 copy.91
  75.4 7.9 %fusion.41 = f32[256,4096]{1,0:T(8,128)} fusion(bf16[256,1024]{0,1:T(8,128)(2,1)} %bitcast.116, bf16[1024,4096]{1,0:T(8,128)(2,1)} %param.8), kind=kOutput, calls=%fused_computation.69 | convolution fusion | flops 2147483648 | bytes 13107200 | tf_op jit(solution)/shard_map/dot_general | solution.py:59
  83.3 3.8 %all-to-all-start = ((bf16[256,8,512]{0,2,1:T(8,128)(2,1)}), bf16[256,8,512]{0,2,1:T(8,128)(2,1)S(1)}, u32[]{:S(2)}, u32[]{:S(2)}) async-start(bf16[256,8,512]{0,2,1:T(8,128)(2,1)} %bitcast.15), calls=%async_computation.1 | async-start | bytes 4194304 | tf_op jit(solution)/shard_map/all_to_all | solution.py:105
  87.2 34.3 %all-to-all-done = bf16[256,8,512]{0,2,1:T(8,128)(2,1)S(1)} async-done(((bf16[256,8,512]{0,2,1:T(8,128)(2,1)}), bf16[256,8,512]{0,2,1:T(8,128)(2,1)S(1)}, u32[]{:S(2)}, u32[]{:S(2)}) %all-to-all-start) | async-done | bytes 2097184 | tf_op jit(solution)/shard_map/all_to_all | solution.py:105
  121.5 2.5 copy.95
  124.0 1.7 select_convert_fusion
  125.7 1.9 convolution_bitcast_fusion.4
  128.2 1.0 copy.96
  129.2 1.3 fusion.42
  130.5 1.6 convolution_bitcast_fusion.3
  132.2 3.1 %multiply_reduce_fusion = f32[8,128,128]{2,1,0:T(8,128)S(1)} fusion(f32[8,8,128,128]{3,2,1,0:T(8,128)} %bitcast.118, f32[8]{0:T(128)S(1)} %compare_convert_fusion), kind=kLoop, calls=%fused_computation | loop fusion | flops 1966080 | bytes 4718624 | tf_op jit(solution)/shard_map/reduce_sum | solution.py:23
  135.4 1.5 fusion.5
  136.8 2.0 copy.98
  139.5 1.0 copy.97
  140.5 23.4 %all-gather.8.cloned.1.call-done = bf16[2048,1024]{0,1:T(8,128)(2,1)} async-done(((bf16[256,1024]{0,1:T(8,128)(2,1)}), bf16[2048,1024]{0,1:T(8,128)(2,1)}) %all-gather.8.cloned.1.call-update) | async-done | bytes 4194320 | tf_op jit(solution)/shard_map/all_gather | solution.py:107
  163.9 6.5 %fusion.43 = f32[1024,512]{1,0:T(8,128)} fusion(bf16[2048,1024]{0,1:T(8,128)(2,1)} %all-gather.8.cloned.1.call-done, bf16[2048,512]{1,0:T(8,128)(2,1)} %bitcast.123), kind=kOutput, calls=%fused_computation.71 | convolution fusion | flops 2147483648 | bytes 8388608 | tf_op jit(solution)/shard_map/dot_general | solution.py:106
  170.4 72.5 %reduce-scatter.2.cloned.1.call-done = f32[256,1024]{1,0:T(8,128)} async-done(((f32[256,4096]{1,0:T(8,128)}), f32[256,1024]{1,0:T(8,128)}) %reduce-scatter.2.cloned.1.call-update) | async-done | bytes 1048592 | tf_op jit(solution)/shard_map/reduce_scatter | solution.py:60
  242.8 2.1 convert_element_type.48
  (59 shorter events, 4.2 us)
Async XLA Ops:
  7.2 36.4 %copy-start = (bf16[256,1024]{1,0:T(8,128)(2,1)S(1)}, bf16[256,1024]{1,0:T(8,128)(2,1)}, u32[]{:S(2)}) copy-start(bf16[256,1024]{1,0:T(8,128)(2,1)} %param.5) | copy-start | bytes 1572868
  7.2 36.4 %copy-start.10 = (bf16[256,1024]{1,0:T(8,128)(2,1)S(1)}, bf16[256,1024]{1,0:T(8,128)(2,1)}, u32[]{:S(2)}) copy-start(bf16[256,1024]{1,0:T(8,128)(2,1)} %param.6) | copy-start | bytes 1572868
  7.2 36.8 %copy-start.1 = (bf16[256,1024]{1,0:T(8,128)(2,1)S(1)}, bf16[256,1024]{1,0:T(8,128)(2,1)}, u32[]{:S(2)}) copy-start(bf16[256,1024]{1,0:T(8,128)(2,1)} %param.7) | copy-start | bytes 1572868
  7.2 4.1 %copy-start.14 = (bf16[256,1024]{1,0:T(8,128)(2,1)S(1)}, bf16[256,1024]{1,0:T(8,128)(2,1)}, u32[]{:S(2)}) copy-start(bf16[256,1024]{1,0:T(8,128)(2,1)} %param.9) | copy-start | bytes 1572868
  7.2 54.5 %all-gather.4.cloned.1.call-start = ((), (), s32[]{:S(2)}) async-start(), calls=%async_computation.2 | async-start | bytes 4718592 | tf_op jit(solution)/shard_map/all_gather | solution.py:50
  8.9 35.7 %copy-start.3 = (bf16[256,8,128]{0,2,1:T(8,128)(2,1)}, bf16[256,8,128]{0,2,1:T(8,128)(2,1)S(1)}, u32[]{:S(2)}) copy-start(bf16[256,8,128]{0,2,1:T(8,128)(2,1)S(1)} %copy.77) | copy-start | bytes 1572868
  11.2 120.9 %all-gather.6.cloned.1.call-start = ((), (), s32[]{:S(2)}) async-start(), calls=%async_computation.4 | async-start | bytes 4718592 | tf_op jit(solution)/shard_map/all_gather | solution.py:85
  11.5 17.1 %collective-permute-start = (bf16[256,1024]{0,1:T(8,128)(2,1)S(1)}, bf16[256,1024]{0,1:T(8,128)(2,1)S(1)}, u32[]{:S(2)}, u32[]{:S(2)}) collective-permute-start(bf16[256,1024]{0,1:T(8,128)(2,1)S(1)} %copy.81), channel_id=1, source_target_pairs={{0,1},{1,2},{2,3},{3,0},{4,5},{5,6},{6,7},{7,4},{8,9},{9,10},{10,1... | collective-permute-start | bytes 1572872 | tf_op jit(solution)/shard_map/ppermute | solution.py:65
  28.6 15.0 %copy-start.12 = (bf16[256,1024]{0,1:T(8,128)(2,1)}, bf16[256,1024]{0,1:T(8,128)(2,1)S(1)}, u32[]{:S(2)}) copy-start(bf16[256,1024]{0,1:T(8,128)(2,1)S(1)} %collective-permute-done) | copy-start | bytes 1572868
  28.6 15.0 %collective-permute-start.1 = (bf16[256,1024]{0,1:T(8,128)(2,1)S(1)}, bf16[256,1024]{0,1:T(8,128)(2,1)}, u32[]{:S(2)}, u32[]{:S(2)}) collective-permute-start(bf16[256,1024]{0,1:T(8,128)(2,1)S(1)} %collective-permute-done), channel_id=1, source_target_pairs={{0,1},{1,2},{2,3},{3,0},{4,5},{5,6},{6,7},{7,4},{8,9},{9,10},{10,1... | collective-permute-start | bytes 1572872 | tf_op jit(solution)/shard_map/ppermute | solution.py:65
  43.5 14.2 %collective-permute-start.2 = (bf16[256,1024]{0,1:T(8,128)(2,1)}, bf16[256,1024]{0,1:T(8,128)(2,1)S(1)}, u32[]{:S(2)}, u32[]{:S(2)}) collective-permute-start(bf16[256,1024]{0,1:T(8,128)(2,1)} %collective-permute-done.1), channel_id=1, source_target_pairs={{0,1},{1,2},{2,3},{3,0},{4,5},{5,6},{6,7},{7,4},{8,9},{9,10},{10,1... | collective-permute-start | bytes 1572872 | tf_op jit(solution)/shard_map/ppermute | solution.py:65
  44.0 16.1 %copy-start.6 = (bf16[8,256,256]{2,1,0:T(8,128)(2,1)}, bf16[8,256,256]{2,1,0:T(8,128)(2,1)S(1)}, u32[]{:S(2)}) copy-start(bf16[8,256,256]{2,1,0:T(8,128)(2,1)S(1)} %select_convert_fusion.1) | copy-start | bytes 3145732
  44.0 14.9 %copy-start.13 = (bf16[256,1024]{0,1:T(8,128)(2,1)S(1)}, bf16[256,1024]{0,1:T(8,128)(2,1)}, u32[]{:S(2)}) copy-start(bf16[256,1024]{0,1:T(8,128)(2,1)} %copy-done.12) | copy-start | bytes 1572868
  64.5 0.8 copy-start.4
  74.6 89.2 %all-gather.8.cloned.1.call-start = ((), (), s32[]{:S(2)}) async-start(), calls=%async_computation.5 | async-start | bytes 4718592 | tf_op jit(solution)/shard_map/all_gather | solution.py:107
  75.4 167.5 %reduce-scatter.2.cloned.1.call-start = ((), (), s32[]{:S(2)}) async-start(), calls=%async_computation.3 | async-start | bytes 5242880 | tf_op jit(solution)/shard_map/reduce_scatter | solution.py:60
  83.3 38.2 %all-to-all-start = ((bf16[256,8,512]{0,2,1:T(8,128)(2,1)}), bf16[256,8,512]{0,2,1:T(8,128)(2,1)S(1)}, u32[]{:S(2)}, u32[]{:S(2)}) async-start(bf16[256,8,512]{0,2,1:T(8,128)(2,1)} %bitcast.15), calls=%async_computation.1 | async-start | bytes 4194304 | tf_op jit(solution)/shard_map/all_to_all | solution.py:105
  124.0 3.6 %copy-start.5 = (f32[8,128,128]{2,1,0:T(8,128)S(1)}, f32[8,128,128]{2,1,0:T(8,128)}, u32[]{:S(2)}) copy-start(f32[8,128,128]{2,1,0:T(8,128)} %copy-done.4) | copy-start | bytes 1572868
  124.0 5.3 %copy-start.7 = (bf16[8,256,256]{2,1,0:T(8,128)(2,1)S(1)}, bf16[8,256,256]{2,1,0:T(8,128)(2,1)}, u32[]{:S(2)}) copy-start(bf16[8,256,256]{2,1,0:T(8,128)(2,1)} %copy-done.6) | copy-start | bytes 3145732
  125.7 2.5 %copy-start.8 = (bf16[8,256,256]{2,1,0:T(8,128)(2,1)}, bf16[8,256,256]{2,1,0:T(8,128)(2,1)S(1)}, u32[]{:S(2)}) copy-start(bf16[8,256,256]{2,1,0:T(8,128)(2,1)S(1)} %select_convert_fusion) | copy-start | bytes 3145732
  130.5 4.8 %copy-start.11 = (bf16[256,1024]{1,0:T(8,128)(2,1)S(1)}, bf16[256,1024]{1,0:T(8,128)(2,1)}, u32[]{:S(2)}) copy-start(bf16[256,1024]{1,0:T(8,128)(2,1)} %param.6) | copy-start | bytes 1572868
  132.2 3.2 %copy-start.9 = (f32[8,128,256]{2,1,0:T(8,128)S(1)}, f32[8,128,256]{2,1,0:T(8,128)}, u32[]{:S(2)}) copy-start(f32[8,128,256]{2,1,0:T(8,128)} %fusion.42) | copy-start | bytes 3145732
  132.2 6.7 %copy-start.2 = (bf16[256,1024]{1,0:T(8,128)(2,1)S(1)}, bf16[256,1024]{1,0:T(8,128)(2,1)}, u32[]{:S(2)}) copy-start(bf16[256,1024]{1,0:T(8,128)(2,1)} %param.7) | copy-start | bytes 1572868
Sparse Core Ops, SparseCore 0:
  11.4 39.2 all-gather.3
  74.7 50.6 all-gather.5
  127.9 35.8 all-gather.7
  166.0 76.7 reduce-scatter.1
